TPU v7x, 32 devices: a whole 2x2x4 slice. The times are simulated.
32 devices in a mesh: shots: 2 (over x), slab: 16 (over z, y, core).
Axes of the slice: x: 2, y: 2, z: 4, core: 2. Of those that a mesh axis runs over, the one named last changes fastest.
Arguments:
- fields: float32 [32, 2, 2, 128, 256], P(('shots', 'slab')), parts along dimension 0, may hold values from -6 to 6
- freq_index: int32 [32], P(('shots', 'slab')), parts along dimension 0, may hold values from 0 to 511
- slowness_index: int32 [16, 128, 256], P('slab'), may hold values from 0 to 255
- slowness_table: float32 [256], replicated, may hold values from 1.2 to 2.4
Outputs:
- image: float32 [32, 128, 256], P(('shots', 'slab')), parts along dimension 0
- fields_out: float32 [32, 2, 2, 128, 256], P(('shots', 'slab')), parts along dimension 0
There are 2 independent parts, one for each index of `shots`. A program takes and returns all parts, laid end to end along the dimension named above; an argument that names none is the same for every part. Nothing has to cross between parts.
All inputs are finite; a program needn't handle non-finite values.
Results may differ from a plain program's by a relative error of at most 0.0003.
Values sent between devices are 32-bit elements; how exact they have to be, the bound alone decides.
A program may use at most 64 MiB of HBM per device.

v0:
```python
import functools
import math

import jax
import jax.numpy as jnp
import numpy as np
from jax import lax
from jax.experimental import pallas as pl
from jax.experimental.pallas import tpu as pltpu
from jax.sharding import PartitionSpec as P

TICKS = 3
NFREQ = 512

F32 = jnp.float32
BF16 = jnp.bfloat16
PI_HI = 3.140625
PI_LO = math.pi - 3.140625


def split_np(mat):
    high = mat.astype(BF16)
    low = (mat - high.astype(np.float64)).astype(BF16)
    return high, low


def dft_tables(nx, ny):
    half = ny // 2
    turn = np.outer(np.arange(nx), np.arange(nx)) % nx * (2.0 * np.pi / nx)
    c, s = np.cos(turn), np.sin(turn)
    x_mats = [np.block([[c, s], [-s, c]]), np.block([[c, -s], [s, c]]) / nx]
    y_mats = []
    for odd in (0, 1):
        turn = np.outer(np.arange(half), 2 * np.arange(half) + odd) % ny * (2.0 * np.pi / ny)
        c, s = np.cos(turn), np.sin(turn)
        y_mats.append(np.block([[c, -s], [s, c]]))
        y_mats.append(np.block([[c.T, s.T], [-s.T, c.T]]) / ny)
    xs = np.stack([part for mat in x_mats for part in split_np(mat)])
    ys = np.stack([part for mat in y_mats for part in split_np(mat)])
    return xs, ys


def split(value):
    high = value.astype(BF16)
    low = (value - high.astype(F32)).astype(BF16)
    return high, low


def dot_data_left(data, high, low):
    d_high, d_low = split(data)
    left = jnp.concatenate([d_high, d_low, d_high], axis=1)
    right = jnp.concatenate([high, high, low], axis=0)
    return jnp.dot(left, right, preferred_element_type=F32)


def dot_data_right(high, low, data):
    d_high, d_low = split(data)
    left = jnp.concatenate([high, high, low], axis=1)
    right = jnp.concatenate([d_high, d_low, d_high], axis=0)
    return jnp.dot(left, right, preferred_element_type=F32)


def sincos(x):
    turns = jnp.floor(x * (1.0 / math.pi) + 0.5)
    r = (x - turns * PI_HI) - turns * PI_LO
    sign = 1.0 - 2.0 * (turns - 2.0 * jnp.floor(turns * 0.5))
    r2 = r * r
    sin_p = 1.0 / math.factorial(11) * -1.0
    for k, sg in ((9, 1.0), (7, -1.0), (5, 1.0), (3, -1.0)):
        sin_p = sin_p * r2 + sg / math.factorial(k)
    sin_p = r + r * (r2 * sin_p)
    cos_p = 1.0 / math.factorial(12)
    for k, sg in ((10, -1.0), (8, 1.0), (6, -1.0), (4, 1.0), (2, -1.0), (0, 1.0)):
        cos_p = cos_p * r2 + sg / math.factorial(k)
    return sign * sin_p, sign * cos_p


def kernel(
    count, fields, freq, sidx, table, xs_in, ys_in, image_out, fields_out,
    held, made, plane, index, levels, xs, ys, raw, low, high, omegas,
    in_sems, send_sems, recv_sems, om_send, om_recv, im_send, im_recv, out_sems,
):
    me = lax.axis_index("slab")
    nx, ny = plane.shape
    half = ny // 2
    has_next = me < count - 1
    has_prev = me > 0
    nxt = jnp.minimum(me + 1, count - 1)
    prv = jnp.maximum(me - 1, 0)

    loads = [
        pltpu.make_async_copy(table, levels, in_sems.at[0]),
        pltpu.make_async_copy(sidx.at[0], index, in_sems.at[1]),
        pltpu.make_async_copy(xs_in, xs, in_sems.at[2]),
        pltpu.make_async_copy(fields.at[0, 0], held.at[0, 0], in_sems.at[3]),
        pltpu.make_async_copy(ys_in, ys, in_sems.at[4]),
        pltpu.make_async_copy(fields.at[0, 1], held.at[0, 1], in_sems.at[5]),
    ]
    for load in loads:
        load.start()

    barrier = pltpu.get_barrier_semaphore()

    @pl.when(has_next)
    def _():
        pl.semaphore_signal(barrier, inc=1, device_id={"slab": nxt})

    @pl.when(has_prev)
    def _():
        pl.semaphore_signal(barrier, inc=1, device_id={"slab": prv})

    def field_copy(tick, f):
        return pltpu.make_async_remote_copy(
            src_ref=made.at[tick, f], dst_ref=held.at[tick + 1, f],
            send_sem=send_sems.at[tick, f], recv_sem=recv_sems.at[tick, f],
            device_id={"slab": nxt},
        )

    def omega_copy(tick):
        return pltpu.make_async_remote_copy(
            src_ref=omegas.at[tick], dst_ref=omegas.at[tick + 1],
            send_sem=om_send.at[tick], recv_sem=om_recv.at[tick],
            device_id={"slab": nxt},
        )

    def image_copy(up):
        return pltpu.make_async_remote_copy(
            src_ref=raw, dst_ref=high if up else low,
            send_sem=im_send.at[up], recv_sem=im_recv.at[up],
            device_id={"slab": prv if up else nxt},
        )

    omegas[0] = jnp.full((8, 128), 1.0 + freq[0].astype(F32) / NFREQ, F32)

    pl.semaphore_wait(barrier, (nxt - me) + (me - prv))

    @pl.when(has_next)
    def _():
        omega_copy(0).start()

    @pl.when(jnp.logical_not(has_prev))
    def _():
        held[1:] = jnp.zeros((TICKS - 1,) + held.shape[1:], F32)
        omegas[1:] = jnp.zeros((TICKS - 1, 8, 128), F32)
        low[...] = jnp.zeros((nx, ny), F32)

    @pl.when(jnp.logical_not(has_next))
    def _():
        high[...] = jnp.zeros((nx, ny), F32)

    loads[0].wait()
    loads[1].wait()
    pieces = [
        jnp.broadcast_to(levels[pl.ds(j * 128, 128)].reshape(1, 128), (nx, 128))
        for j in range(levels.shape[0] // 128)
    ]
    for h in range(ny // 128):
        cols = pl.ds(h * 128, 128)
        idx = index[:, cols]
        inner = idx & 127
        value = jnp.take_along_axis(pieces[0], inner, axis=1, mode="promise_in_bounds")
        for j in range(1, len(pieces)):
            other = jnp.take_along_axis(pieces[j], inner, axis=1, mode="promise_in_bounds")
            value = jnp.where(idx >= j * 128, other, value)
        plane[:, cols] = value
    mean_slow = jnp.sum(plane[...]) * (1.0 / (nx * ny))

    row = lax.broadcasted_iota(jnp.int32, (nx, half), 0)
    wave_x = jnp.where(row < (nx + 1) // 2, row, row - nx).astype(F32) * (2.0 * math.pi / nx)
    lane = lax.broadcasted_iota(jnp.int32, (1, half), 1)

    def phases(omega):
        k_square = (omega * mean_slow) ** 2
        out = []
        for odd in (0, 1):
            k = 2 * lane + odd
            wave_y = jnp.where(k < (ny + 1) // 2, k, k - ny).astype(F32) * (2.0 * math.pi / ny)
            q = k_square - (wave_x * wave_x + wave_y * wave_y)
            root = jnp.sqrt(jnp.abs(q))
            sin_v, cos_v = sincos(root)
            moving = q > 0.0
            out.append((
                jnp.where(moving, cos_v, jnp.exp(-root)),
                jnp.where(moving, sin_v, 0.0),
            ))
        return out

    def step(tick, f, phase, screen):
        re, im = held[tick, f, 0], held[tick, f, 1]
        sg = 1.0 if f == 0 else -1.0
        spec = dot_data_right(xs[0], xs[1], jnp.concatenate([re, im], axis=0))
        left, right = spec[:, :half], spec[:, half:]
        back = []
        for odd, mix in ((0, left + right), (1, left - right)):
            cos_p, sin_p = phase[odd]
            sin_p = sg * sin_p
            fwd = dot_data_left(
                jnp.concatenate([mix[:nx], mix[nx:]], axis=1), ys[4 * odd], ys[4 * odd + 1]
            )
            v_re, v_im = fwd[:, :half], fwd[:, half:]
            moved = jnp.concatenate(
                [v_re * cos_p - v_im * sin_p, v_re * sin_p + v_im * cos_p], axis=1
            )
            back.append(dot_data_left(moved, ys[4 * odd + 2], ys[4 * odd + 3]))
        plus, minus = back[0] + back[1], back[0] - back[1]
        cols = jnp.concatenate([
            jnp.concatenate([plus[:, :half], minus[:, :half]], axis=1),
            jnp.concatenate([plus[:, half:], minus[:, half:]], axis=1),
        ], axis=0)
        field = dot_data_right(xs[2], xs[3], cols)
        b_re, b_im = field[:nx], field[nx:]
        s_sin, s_cos = screen
        s_sin = sg * s_sin
        made[tick, f, 0] = b_re * s_cos - b_im * s_sin
        made[tick, f, 1] = b_re * s_sin + b_im * s_cos

    def write_out(f):
        return pltpu.make_async_copy(made.at[TICKS - 1, f], fields_out.at[0, f], out_sems.at[f])

    for tick in range(TICKS):
        if tick > 0:
            @pl.when(has_prev)
            def _():
                omega_copy(tick - 1).wait_recv()

            if tick < TICKS - 1:
                @pl.when(has_next)
                def _():
                    omega_copy(tick).start()
        omega = omegas[tick][:1]
        phase = phases(omega)
        omega_wide = jnp.concatenate([omega] * (ny // 128), axis=1)
        screen = sincos(omega_wide * (plane[...] - mean_slow))
        if tick == 0:
            loads[2].wait()
        for f in (0, 1):
            if tick == 0:
                loads[3 + 2 * f].wait()
                if f == 0:
                    loads[4].wait()
            else:
                @pl.when(has_prev)
                def _():
                    field_copy(tick - 1, f).wait_recv()
            step(tick, f, phase, screen)
            if tick < TICKS - 1:
                @pl.when(has_next)
                def _():
                    field_copy(tick, f).start()
            else:
                write_out(f).start()
        added = made[tick, 0, 0] * made[tick, 1, 0] + made[tick, 0, 1] * made[tick, 1, 1]
        raw[...] = added if tick == 0 else raw[...] + added

    @pl.when(has_next)
    def _():
        image_copy(0).start()

    @pl.when(has_prev)
    def _():
        image_copy(1).start()

    @pl.when(has_prev)
    def _():
        image_copy(0).wait_recv()

    @pl.when(has_next)
    def _():
        image_copy(1).wait_recv()

    plane[...] = raw[...] - 0.25 * (low[...] + high[...])
    last = pltpu.make_async_copy(plane, image_out.at[0], out_sems.at[2])
    last.start()

    @pl.when(has_next)
    def _():
        for tick in range(TICKS - 1):
            omega_copy(tick).wait_send()
            for f in (0, 1):
                field_copy(tick, f).wait_send()
        image_copy(0).wait_send()

    @pl.when(has_prev)
    def _():
        image_copy(1).wait_send()

    write_out(0).wait()
    write_out(1).wait()
    last.wait()


def body(fields, freq_index, slowness_index, slowness_table):
    nx, ny = slowness_index.shape[1:]
    assert slowness_index.shape[0] == 1
    xs, ys = dft_tables(nx, ny)
    count = lax.axis_size("slab")
    any_spec = pl.BlockSpec(memory_space=pl.ANY)
    return pl.pallas_call(
        functools.partial(kernel, count),
        out_shape=(
            jax.ShapeDtypeStruct((1, nx, ny), F32),
            jax.ShapeDtypeStruct(fields.shape, F32),
        ),
        in_specs=[
            any_spec, pl.BlockSpec(memory_space=pltpu.SMEM), any_spec, any_spec, any_spec, any_spec,
        ],
        out_specs=(any_spec, any_spec),
        scratch_shapes=[
            pltpu.VMEM((TICKS, 2, 2, nx, ny), F32),
            pltpu.VMEM((TICKS, 2, 2, nx, ny), F32),
            pltpu.VMEM((nx, ny), F32),
            pltpu.VMEM((nx, ny), jnp.int32),
            pltpu.VMEM(slowness_table.shape, F32),
            pltpu.VMEM(xs.shape, BF16),
            pltpu.VMEM(ys.shape, BF16),
            pltpu.VMEM((nx, ny), F32),
            pltpu.VMEM((nx, ny), F32),
            pltpu.VMEM((nx, ny), F32),
            pltpu.VMEM((TICKS, 8, 128), F32),
            pltpu.SemaphoreType.DMA((6,)),
            pltpu.SemaphoreType.DMA((TICKS - 1, 2)),
            pltpu.SemaphoreType.DMA((TICKS - 1, 2)),
            pltpu.SemaphoreType.DMA((TICKS - 1,)),
            pltpu.SemaphoreType.DMA((TICKS - 1,)),
            pltpu.SemaphoreType.DMA((2,)),
            pltpu.SemaphoreType.DMA((2,)),
            pltpu.SemaphoreType.DMA((3,)),
        ],
        compiler_params=pltpu.CompilerParams(collective_id=0, has_side_effects=True),
        name="slabs",
    )(fields, freq_index, slowness_index, slowness_table, jnp.asarray(xs), jnp.asarray(ys))


def solution(mesh):
    return jax.shard_map(
        body,
        mesh=mesh,
        in_specs=(
            P(("shots", "slab"), None, None, None, None),
            P(("shots", "slab")),
            P("slab", None, None),
            P(),
        ),
        out_specs=(P(("shots", "slab"), None, None), P(("shots", "slab"), None, None, None, None)),
        check_vma=False,
    )
```

profile of v0, /device:TPU:15, one launch (start us, length us, event | category | flops | bytes accessed | tf_op | source)
XLA Modules:
  0.0 28.4 jit_solution(7464672132856052565)
XLA Ops:
  1.3 23.7 %slabs.1 = (f32[1,128,256]{2,1,0:T(8,128)}, f32[1,2,2,128,256]{4,3,2,1,0:T(8,128)}) custom-call(f32[1,2,2,128,256]{4,3,2,1,0:T(8,128)} %fields.1, s32[1]{0:T(128)S(6)} %copy.10.freq, s32[1,128,256]{2,1,0:T(8,128)} %sidx.1, f32[256]{0:T(256)} %table.1, bf16[4,256,256]{2,1,0:T(8,128)(2,1)} %constant.4.clone.xs_in, bf16[8,256,256]{2,1,0:T(8,128)(2,1)} %constant.5.clone.ys_in), custom_call_target="tpu_custom_call" | custom-call | tf_op jit(solution)/shard_map/slabs/pallas_call | solution.py:298
  25.0 1.6 %copy.11 = f32[1,128,256]{2,1,0:T(8,128)} copy(f32[1,128,256]{2,1,0:T(8,128)} %get-tuple-element.4) | data formatting | bytes 262144
  26.5 1.9 %copy.12 = f32[1,2,2,128,256]{4,3,2,1,0:T(8,128)} copy(f32[1,2,2,128,256]{4,3,2,1,0:T(8,128)} %get-tuple-element.5) | data formatting | bytes 1048576
where the time goes:
time: 28.6 us; the launch traced here: 28.4 us
  Pallas kernels  23.7 us (83%)
  local copies, waits for them, and re-layouts  3.44 us (12%)
  between operations  1.28 us (4%)
    pallas_call x1, Pallas kernels, body(): pl.pallas_call(functools.partial(kernel, count), out_shape=(jax.ShapeDtyp...  23.7 us
    unnamed x2, local copies, waits for them, and re-layouts  3.44 us

commit v1 on v0

--- a/solution.py
+++ b/solution.py
@@ -78,7 +78,7 @@
 def kernel(
     count, fields, freq, sidx, table, xs_in, ys_in, image_out, fields_out,
     held, made, plane, index, levels, xs, ys, raw, low, high, omegas,
-    in_sems, send_sems, recv_sems, om_send, om_recv, im_send, im_recv, out_sems,
+    in_sems, send_sems, recv_sems, om_send, om_recv, im_send, im_recv,
 ):
     me = lax.axis_index("slab")
     nx, ny = plane.shape
@@ -211,11 +211,12 @@
         b_re, b_im = field[:nx], field[nx:]
         s_sin, s_cos = screen
         s_sin = sg * s_sin
-        made[tick, f, 0] = b_re * s_cos - b_im * s_sin
-        made[tick, f, 1] = b_re * s_sin + b_im * s_cos
-
-    def write_out(f):
-        return pltpu.make_async_copy(made.at[TICKS - 1, f], fields_out.at[0, f], out_sems.at[f])
+        target = moved_fields(tick)
+        target[f, 0] = b_re * s_cos - b_im * s_sin
+        target[f, 1] = b_re * s_sin + b_im * s_cos
+
+    def moved_fields(tick):
+        return made.at[tick] if tick < TICKS - 1 else fields_out.at[0]
 
     for tick in range(TICKS):
         if tick > 0:
@@ -247,9 +248,8 @@
                 @pl.when(has_next)
                 def _():
                     field_copy(tick, f).start()
-            else:
-                write_out(f).start()
-        added = made[tick, 0, 0] * made[tick, 1, 0] + made[tick, 0, 1] * made[tick, 1, 1]
+        now = moved_fields(tick)
+        added = now[0, 0] * now[1, 0] + now[0, 1] * now[1, 1]
         raw[...] = added if tick == 0 else raw[...] + added
 
     @pl.when(has_next)
@@ -268,9 +268,7 @@
     def _():
         image_copy(1).wait_recv()
 
-    plane[...] = raw[...] - 0.25 * (low[...] + high[...])
-    last = pltpu.make_async_copy(plane, image_out.at[0], out_sems.at[2])
-    last.start()
+    image_out[0] = raw[...] - 0.25 * (low[...] + high[...])
 
     @pl.when(has_next)
     def _():
@@ -284,9 +282,16 @@
     def _():
         image_copy(1).wait_send()
 
-    write_out(0).wait()
-    write_out(1).wait()
-    last.wait()
+
+def store(image, fields, image_out, fields_out, sems):
+    copies = [
+        pltpu.make_async_copy(fields, fields_out, sems.at[0]),
+        pltpu.make_async_copy(image, image_out, sems.at[1]),
+    ]
+    for copy in copies:
+        copy.start()
+    for copy in copies:
+        copy.wait()
 
 
 def body(fields, freq_index, slowness_index, slowness_table):
@@ -295,19 +300,17 @@
     xs, ys = dft_tables(nx, ny)
     count = lax.axis_size("slab")
     any_spec = pl.BlockSpec(memory_space=pl.ANY)
-    return pl.pallas_call(
+    vmem_spec = pl.BlockSpec(memory_space=pltpu.VMEM)
+    image, moved = pl.pallas_call(
         functools.partial(kernel, count),
-        out_shape=(
-            jax.ShapeDtypeStruct((1, nx, ny), F32),
-            jax.ShapeDtypeStruct(fields.shape, F32),
-        ),
+        out_shape=(pltpu.VMEM((1, nx, ny), F32), pltpu.VMEM(fields.shape, F32)),
         in_specs=[
             any_spec, pl.BlockSpec(memory_space=pltpu.SMEM), any_spec, any_spec, any_spec, any_spec,
         ],
-        out_specs=(any_spec, any_spec),
+        out_specs=(vmem_spec, vmem_spec),
         scratch_shapes=[
             pltpu.VMEM((TICKS, 2, 2, nx, ny), F32),
-            pltpu.VMEM((TICKS, 2, 2, nx, ny), F32),
+            pltpu.VMEM((TICKS - 1, 2, 2, nx, ny), F32),
             pltpu.VMEM((nx, ny), F32),
             pltpu.VMEM((nx, ny), jnp.int32),
             pltpu.VMEM(slowness_table.shape, F32),
@@ -324,11 +327,24 @@
             pltpu.SemaphoreType.DMA((TICKS - 1,)),
             pltpu.SemaphoreType.DMA((2,)),
             pltpu.SemaphoreType.DMA((2,)),
-            pltpu.SemaphoreType.DMA((3,)),
         ],
         compiler_params=pltpu.CompilerParams(collective_id=0, has_side_effects=True),
         name="slabs",
     )(fields, freq_index, slowness_index, slowness_table, jnp.asarray(xs), jnp.asarray(ys))
+    return pl.pallas_call(
+        store,
+        out_shape=(
+            jax.ShapeDtypeStruct((1, nx, ny), F32),
+            jax.ShapeDtypeStruct(fields.shape, F32),
+        ),
+        in_specs=[vmem_spec, vmem_spec],
+        out_specs=(any_spec, any_spec),
+        scratch_shapes=[pltpu.SemaphoreType.DMA((2,))],
+        name="store",
+    )(
+        pltpu.with_memory_space_constraint(image, pltpu.VMEM),
+        pltpu.with_memory_space_constraint(moved, pltpu.VMEM),
+    )
 
 
 def solution(mesh):

time: 28.6 us -> 25.3 us (0.88)
  the two profiles are of different devices: /device:TPU:15 before, /device:TPU:7 now
where the time goes in v1:
time: 25.3 us; the launch traced here: 25.1 us
  Pallas kernels  23.8 us (94%)
  between operations  1.28 us (5%)
    pallas_call x1, Pallas kernels, body(): pl.pallas_call(functools.partial(kernel, count), out_shape=(pltpu.VMEM((1...  23 us
    pallas_call x1, Pallas kernels, body(): pl.pallas_call(store, out_shape=(jax.ShapeDtypeStruct((1, nx, ny), F32),...  0.85 us

profile of v1, /device:TPU:7, one launch (start us, length us, event | category | flops | bytes accessed | tf_op | source)
XLA Modules:
  0.0 25.1 jit_solution(15156917795986587322)
XLA Ops:
  1.3 23.0 %slabs.1 = (f32[1,128,256]{2,1,0:T(8,128)S(1)}, f32[1,2,2,128,256]{4,3,2,1,0:T(8,128)S(1)}) custom-call(f32[1,2,2,128,256]{4,3,2,1,0:T(8,128)} %fields.1, s32[1]{0:T(128)S(6)} %copy.8.freq, s32[1,128,256]{2,1,0:T(8,128)} %sidx.1, f32[256]{0:T(256)} %table.1, bf16[4,256,256]{2,1,0:T(8,128)(2,1)} %constant.4.clone.xs_in, bf16[8,256,256]{2,1,0:T(8,128)(2,1)} %constant.5.clone.ys_in), custom_call_target="tpu_custom_call" | custom-call | tf_op jit(solution)/shard_map/slabs/pallas_call | solution.py:304
  24.3 0.8 %store.1 = (f32[1,128,256]{2,1,0:T(8,128)}, f32[1,2,2,128,256]{4,3,2,1,0:T(8,128)}) custom-call(f32[1,128,256]{2,1,0:T(8,128)S(1)} %get-tuple-element.4.image, f32[1,2,2,128,256]{4,3,2,1,0:T(8,128)S(1)} %get-tuple-element.5.fields), custom_call_target="tpu_custom_call" | custom-call | tf_op jit(solution)/shard_map/store/pallas_call | solution.py:334

commit v2 on v1

--- a/solution.py
+++ b/solution.py
@@ -78,7 +78,8 @@
 def kernel(
     count, fields, freq, sidx, table, xs_in, ys_in, image_out, fields_out,
     held, made, plane, index, levels, xs, ys, raw, low, high, omegas,
-    in_sems, send_sems, recv_sems, om_send, om_recv, im_send, im_recv,
+    index_next, plane_next, ahead, bonus, part,
+    in_sems, send_sems, recv_sems, om_send, om_recv, im_send, im_recv, ix_send, ix_recv,
 ):
     me = lax.axis_index("slab")
     nx, ny = plane.shape
@@ -87,6 +88,9 @@
     has_prev = me > 0
     nxt = jnp.minimum(me + 1, count - 1)
     prv = jnp.maximum(me - 1, 0)
+    odd = lax.rem(me, 2) == 1
+    looks_ahead = jnp.logical_and(odd, has_next)
+    is_looked = jnp.logical_and(jnp.logical_not(odd), has_prev)
 
     loads = [
         pltpu.make_async_copy(table, levels, in_sems.at[0]),
@@ -123,9 +127,15 @@
             device_id={"slab": nxt},
         )
 
-    def image_copy(up):
+    def index_copy():
         return pltpu.make_async_remote_copy(
-            src_ref=raw, dst_ref=high if up else low,
+            src_ref=sidx.at[0], dst_ref=index_next,
+            send_sem=ix_send, recv_sem=ix_recv, device_id={"slab": prv},
+        )
+
+    def image_copy(up, source=raw):
+        return pltpu.make_async_remote_copy(
+            src_ref=source, dst_ref=high if up else low,
             send_sem=im_send.at[up], recv_sem=im_recv.at[up],
             device_id={"slab": prv if up else nxt},
         )
@@ -133,6 +143,10 @@
     omegas[0] = jnp.full((8, 128), 1.0 + freq[0].astype(F32) / NFREQ, F32)
 
     pl.semaphore_wait(barrier, (nxt - me) + (me - prv))
+
+    @pl.when(is_looked)
+    def _():
+        index_copy().start()
 
     @pl.when(has_next)
     def _():
@@ -154,22 +168,26 @@
         jnp.broadcast_to(levels[pl.ds(j * 128, 128)].reshape(1, 128), (nx, 128))
         for j in range(levels.shape[0] // 128)
     ]
-    for h in range(ny // 128):
-        cols = pl.ds(h * 128, 128)
-        idx = index[:, cols]
-        inner = idx & 127
-        value = jnp.take_along_axis(pieces[0], inner, axis=1, mode="promise_in_bounds")
-        for j in range(1, len(pieces)):
-            other = jnp.take_along_axis(pieces[j], inner, axis=1, mode="promise_in_bounds")
-            value = jnp.where(idx >= j * 128, other, value)
-        plane[:, cols] = value
-    mean_slow = jnp.sum(plane[...]) * (1.0 / (nx * ny))
+
+    def lookup(index, plane):
+        for h in range(ny // 128):
+            cols = pl.ds(h * 128, 128)
+            idx = index[:, cols]
+            inner = idx & 127
+            value = jnp.take_along_axis(pieces[0], inner, axis=1, mode="promise_in_bounds")
+            for j in range(1, len(pieces)):
+                other = jnp.take_along_axis(pieces[j], inner, axis=1, mode="promise_in_bounds")
+                value = jnp.where(idx >= j * 128, other, value)
+            plane[:, cols] = value
+        return jnp.sum(plane[...]) * (1.0 / (nx * ny))
+
+    mean_slow = lookup(index, plane)
 
     row = lax.broadcasted_iota(jnp.int32, (nx, half), 0)
     wave_x = jnp.where(row < (nx + 1) // 2, row, row - nx).astype(F32) * (2.0 * math.pi / nx)
     lane = lax.broadcasted_iota(jnp.int32, (1, half), 1)
 
-    def phases(omega):
+    def phases(omega, mean_slow):
         k_square = (omega * mean_slow) ** 2
         out = []
         for odd in (0, 1):
@@ -185,8 +203,8 @@
             ))
         return out
 
-    def step(tick, f, phase, screen):
-        re, im = held[tick, f, 0], held[tick, f, 1]
+    def step(source, target, f, phase, screen):
+        re, im = source[f, 0], source[f, 1]
         sg = 1.0 if f == 0 else -1.0
         spec = dot_data_right(xs[0], xs[1], jnp.concatenate([re, im], axis=0))
         left, right = spec[:, :half], spec[:, half:]
@@ -211,12 +229,15 @@
         b_re, b_im = field[:nx], field[nx:]
         s_sin, s_cos = screen
         s_sin = sg * s_sin
-        target = moved_fields(tick)
         target[f, 0] = b_re * s_cos - b_im * s_sin
         target[f, 1] = b_re * s_sin + b_im * s_cos
 
     def moved_fields(tick):
         return made.at[tick] if tick < TICKS - 1 else fields_out.at[0]
+
+    def factors(omega, plane, mean_slow):
+        omega_wide = jnp.concatenate([omega] * (ny // 128), axis=1)
+        return phases(omega, mean_slow), sincos(omega_wide * (plane[...] - mean_slow))
 
     for tick in range(TICKS):
         if tick > 0:
@@ -228,10 +249,7 @@
                 @pl.when(has_next)
                 def _():
                     omega_copy(tick).start()
-        omega = omegas[tick][:1]
-        phase = phases(omega)
-        omega_wide = jnp.concatenate([omega] * (ny // 128), axis=1)
-        screen = sincos(omega_wide * (plane[...] - mean_slow))
+        phase, screen = factors(omegas[tick][:1], plane, mean_slow)
         if tick == 0:
             loads[2].wait()
         for f in (0, 1):
@@ -243,7 +261,11 @@
                 @pl.when(has_prev)
                 def _():
                     field_copy(tick - 1, f).wait_recv()
-            step(tick, f, phase, screen)
+            if tick == TICKS - 1 and f == 0:
+                @pl.when(is_looked)
+                def _():
+                    image_copy(1, part).start()
+            step(held.at[tick], moved_fields(tick), f, phase, screen)
             if tick < TICKS - 1:
                 @pl.when(has_next)
                 def _():
@@ -251,24 +273,39 @@
         now = moved_fields(tick)
         added = now[0, 0] * now[1, 0] + now[0, 1] * now[1, 1]
         raw[...] = added if tick == 0 else raw[...] + added
+        if tick == TICKS - 2:
+            part[...] = raw[...]
+
+            @pl.when(looks_ahead)
+            def _():
+                index_copy().wait_recv()
+                mean_next = lookup(index_next, plane_next)
+                phase, screen = factors(omegas[tick][:1], plane_next, mean_next)
+                for f in (0, 1):
+                    step(made.at[tick], ahead, f, phase, screen)
+                bonus[...] = ahead[0, 0] * ahead[1, 0] + ahead[0, 1] * ahead[1, 1]
+
+            @pl.when(jnp.logical_not(looks_ahead))
+            def _():
+                bonus[...] = jnp.zeros((nx, ny), F32)
 
     @pl.when(has_next)
     def _():
         image_copy(0).start()
 
+    @pl.when(odd)
+    def _():
+        image_copy(1).start()
+
     @pl.when(has_prev)
     def _():
-        image_copy(1).start()
-
-    @pl.when(has_prev)
-    def _():
         image_copy(0).wait_recv()
 
     @pl.when(has_next)
     def _():
         image_copy(1).wait_recv()
 
-    image_out[0] = raw[...] - 0.25 * (low[...] + high[...])
+    image_out[0] = raw[...] - 0.25 * (low[...] + (high[...] + bonus[...]))
 
     @pl.when(has_next)
     def _():
@@ -278,9 +315,14 @@
                 field_copy(tick, f).wait_send()
         image_copy(0).wait_send()
 
-    @pl.when(has_prev)
+    @pl.when(odd)
     def _():
         image_copy(1).wait_send()
+
+    @pl.when(is_looked)
+    def _():
+        index_copy().wait_send()
+        image_copy(1, part).wait_send()
 
 
 def store(image, fields, image_out, fields_out, sems):
@@ -320,6 +362,11 @@
             pltpu.VMEM((nx, ny), F32),
             pltpu.VMEM((nx, ny), F32),
             pltpu.VMEM((TICKS, 8, 128), F32),
+            pltpu.VMEM((nx, ny), jnp.int32),
+            pltpu.VMEM((nx, ny), F32),
+            pltpu.VMEM((2, 2, nx, ny), F32),
+            pltpu.VMEM((nx, ny), F32),
+            pltpu.VMEM((nx, ny), F32),
             pltpu.SemaphoreType.DMA((6,)),
             pltpu.SemaphoreType.DMA((TICKS - 1, 2)),
             pltpu.SemaphoreType.DMA((TICKS - 1, 2)),
@@ -327,6 +374,8 @@
             pltpu.SemaphoreType.DMA((TICKS - 1,)),
             pltpu.SemaphoreType.DMA((2,)),
             pltpu.SemaphoreType.DMA((2,)),
+            pltpu.SemaphoreType.DMA,
+            pltpu.SemaphoreType.DMA,
         ],
         compiler_params=pltpu.CompilerParams(collective_id=0, has_side_effects=True),
         name="slabs",

time: 25.3 us -> 22.5 us (0.89)
  the two profiles are of different devices: /device:TPU:7 before, /device:TPU:9 now
where the time goes in v2:
time: 22.5 us; the launch traced here: 22.3 us
  Pallas kernels  21 us (93%)
  between operations  1.28 us (6%)
    pallas_call x1, Pallas kernels, body(): pl.pallas_call(functools.partial(kernel, count), out_shape=(pltpu.VMEM((1...  20.2 us
    pallas_call x1, Pallas kernels, body(): pl.pallas_call(store, out_shape=(jax.ShapeDtypeStruct((1, nx, ny), F32),...  0.85 us

profile of v2, /device:TPU:9, one launch (start us, length us, event | category | flops | bytes accessed | tf_op | source)
XLA Modules:
  0.0 22.3 jit_solution(13837338079076759791)
XLA Ops:
  1.3 20.2 %slabs.1 = (f32[1,128,256]{2,1,0:T(8,128)S(1)}, f32[1,2,2,128,256]{4,3,2,1,0:T(8,128)S(1)}) custom-call(f32[1,2,2,128,256]{4,3,2,1,0:T(8,128)} %fields.1, s32[1]{0:T(128)S(6)} %copy.8.freq, s32[1,128,256]{2,1,0:T(8,128)} %sidx.1, f32[256]{0:T(256)} %table.1, bf16[4,256,256]{2,1,0:T(8,128)(2,1)} %constant.4.clone.xs_in, bf16[8,256,256]{2,1,0:T(8,128)(2,1)} %constant.5.clone.ys_in), custom_call_target="tpu_custom_call" | custom-call | tf_op jit(solution)/shard_map/slabs/pallas_call | solution.py:346
  21.5 0.8 %store.1 = (f32[1,128,256]{2,1,0:T(8,128)}, f32[1,2,2,128,256]{4,3,2,1,0:T(8,128)}) custom-call(f32[1,128,256]{2,1,0:T(8,128)S(1)} %get-tuple-element.4.image, f32[1,2,2,128,256]{4,3,2,1,0:T(8,128)S(1)} %get-tuple-element.5.fields), custom_call_target="tpu_custom_call" | custom-call | tf_op jit(solution)/shard_map/store/pallas_call | solution.py:383

commit v3 on v2

--- a/solution.py
+++ b/solution.py
@@ -76,9 +76,9 @@
 
 
 def kernel(
-    count, fields, freq, sidx, table, xs_in, ys_in, image_out, fields_out,
+    count, fields, freq_in, sidx, table, xs_in, ys_in, image_out, fields_out,
     held, made, plane, index, levels, xs, ys, raw, low, high, omegas,
-    index_next, plane_next, ahead, bonus, part,
+    index_next, plane_next, ahead, bonus, part, freq,
     in_sems, send_sems, recv_sems, om_send, om_recv, im_send, im_recv, ix_send, ix_recv,
 ):
     me = lax.axis_index("slab")
@@ -95,10 +95,11 @@
     loads = [
         pltpu.make_async_copy(table, levels, in_sems.at[0]),
         pltpu.make_async_copy(sidx.at[0], index, in_sems.at[1]),
-        pltpu.make_async_copy(xs_in, xs, in_sems.at[2]),
+        pltpu.make_async_copy(freq_in, freq, in_sems.at[2]),
         pltpu.make_async_copy(fields.at[0, 0], held.at[0, 0], in_sems.at[3]),
-        pltpu.make_async_copy(ys_in, ys, in_sems.at[4]),
-        pltpu.make_async_copy(fields.at[0, 1], held.at[0, 1], in_sems.at[5]),
+        pltpu.make_async_copy(xs_in, xs, in_sems.at[4]),
+        pltpu.make_async_copy(ys_in, ys, in_sems.at[5]),
+        pltpu.make_async_copy(fields.at[0, 1], held.at[0, 1], in_sems.at[6]),
     ]
     for load in loads:
         load.start()
@@ -140,13 +141,14 @@
             device_id={"slab": prv if up else nxt},
         )
 
+    pl.semaphore_wait(barrier, (nxt - me) + (me - prv))
+
+    @pl.when(is_looked)
+    def _():
+        index_copy().start()
+
+    loads[2].wait()
     omegas[0] = jnp.full((8, 128), 1.0 + freq[0].astype(F32) / NFREQ, F32)
-
-    pl.semaphore_wait(barrier, (nxt - me) + (me - prv))
-
-    @pl.when(is_looked)
-    def _():
-        index_copy().start()
 
     @pl.when(has_next)
     def _():
@@ -162,8 +164,8 @@
     def _():
         high[...] = jnp.zeros((nx, ny), F32)
 
-    loads[0].wait()
-    loads[1].wait()
+    for load in (loads[0], loads[1], loads[3], loads[4], loads[5]):
+        load.wait()
     pieces = [
         jnp.broadcast_to(levels[pl.ds(j * 128, 128)].reshape(1, 128), (nx, 128))
         for j in range(levels.shape[0] // 128)
@@ -250,14 +252,10 @@
                 def _():
                     omega_copy(tick).start()
         phase, screen = factors(omegas[tick][:1], plane, mean_slow)
-        if tick == 0:
-            loads[2].wait()
         for f in (0, 1):
-            if tick == 0:
-                loads[3 + 2 * f].wait()
-                if f == 0:
-                    loads[4].wait()
-            else:
+            if tick == 0 and f == 1:
+                loads[6].wait()
+            elif tick > 0:
                 @pl.when(has_prev)
                 def _():
                     field_copy(tick - 1, f).wait_recv()
@@ -347,7 +345,7 @@
         functools.partial(kernel, count),
         out_shape=(pltpu.VMEM((1, nx, ny), F32), pltpu.VMEM(fields.shape, F32)),
         in_specs=[
-            any_spec, pl.BlockSpec(memory_space=pltpu.SMEM), any_spec, any_spec, any_spec, any_spec,
+            any_spec, any_spec, any_spec, any_spec, any_spec, any_spec,
         ],
         out_specs=(vmem_spec, vmem_spec),
         scratch_shapes=[
@@ -367,7 +365,8 @@
             pltpu.VMEM((2, 2, nx, ny), F32),
             pltpu.VMEM((nx, ny), F32),
             pltpu.VMEM((nx, ny), F32),
-            pltpu.SemaphoreType.DMA((6,)),
+            pltpu.SMEM(freq_index.shape, jnp.int32),
+            pltpu.SemaphoreType.DMA((7,)),
             pltpu.SemaphoreType.DMA((TICKS - 1, 2)),
             pltpu.SemaphoreType.DMA((TICKS - 1, 2)),
             pltpu.SemaphoreType.DMA((TICKS - 1,)),

time: 22.5 us -> 22.4 us (level)
  no operation moved by 1% of the time
where the time goes in v3:
time: 22.4 us; the launch traced here: 22.3 us
  Pallas kernels  21 us (94%)
  between operations  1.28 us (6%)
    pallas_call x1, Pallas kernels, body(): pl.pallas_call(functools.partial(kernel, count), out_shape=(pltpu.VMEM((1...  20.1 us
    pallas_call x1, Pallas kernels, body(): pl.pallas_call(store, out_shape=(jax.ShapeDtypeStruct((1, nx, ny), F32),...  0.85 us

profile of v3, /device:TPU:9, one launch (start us, length us, event | category | flops | bytes accessed | tf_op | source)
XLA Modules:
  0.0 22.3 jit_solution(17234955061948881315)
XLA Ops:
  1.3 20.1 %slabs.1 = (f32[1,128,256]{2,1,0:T(8,128)S(1)}, f32[1,2,2,128,256]{4,3,2,1,0:T(8,128)S(1)}) custom-call(f32[1,2,2,128,256]{4,3,2,1,0:T(8,128)} %fields.1, s32[1]{0:T(128)S(6)} %copy.8.freq_in, s32[1,128,256]{2,1,0:T(8,128)} %sidx.1, f32[256]{0:T(256)} %table.1, bf16[4,256,256]{2,1,0:T(8,128)(2,1)} %constant.4.clone.xs_in, ...), custom_call_target="tpu_custom_call" | custom-call | tf_op jit(solution)/shard_map/slabs/pallas_call | solution.py:344
  21.4 0.8 %store.1 = (f32[1,128,256]{2,1,0:T(8,128)}, f32[1,2,2,128,256]{4,3,2,1,0:T(8,128)}) custom-call(f32[1,128,256]{2,1,0:T(8,128)S(1)} %get-tuple-element.4.image, f32[1,2,2,128,256]{4,3,2,1,0:T(8,128)S(1)} %get-tuple-element.5.fields), custom_call_target="tpu_custom_call" | custom-call | tf_op jit(solution)/shard_map/store/pallas_call | solution.py:382
